TPU v7x, 32 devices: a whole 2x2x4 slice. The times are simulated.
32 devices in a mesh: req: 4 (over y, x), seq: 8 (over z, core).
Axes of the slice: x: 2, y: 2, z: 4, core: 2. Of those that a mesh axis runs over, the one named last changes fastest.
Arguments:
- residual: bfloat16 [64, 2048], P(None, ('req', 'seq')), may hold values from -90 to 90
- query_plain: bfloat16 [64, 16, 128], P('req'), may hold values from -6 to 6
- query_rotary: bfloat16 [64, 16, 64], P('req'), may hold values from -110 to 110
- latent_cache: bfloat16 [64, 3072, 512], P('req', 'seq'), may hold values from -9 to 9
- rotary_cache: bfloat16 [64, 64, 3072], P('req', None, 'seq'), may hold values from -4.5 to 4.5
- lengths: int32 [64], P('req'), may hold values from 2 to 3072, as said below
- absorb_key: bfloat16 [16, 128, 512], replicated, may hold values from -0.5 to 0.5
- absorb_value: bfloat16 [16, 512, 128], replicated, may hold values from -0.25 to 0.25
- output_weight: bfloat16 [2048, 2048], P(None, ('req', 'seq')), may hold values from -0.125 to 0.125
- middle_gain: float32 [2048], replicated, may hold values from 0.5 to 1.5
- routes: int32 [64, 6], replicated, may hold values from 0 to 63, all different within a row
- route_weights: float32 [64, 6], replicated, may hold values from 0.05 to 0.45
- gate_weight: bfloat16 [64, 2048, 1408], P('seq', None, 'req'), may hold values from -0.125 to 0.125
- up_weight: bfloat16 [64, 2048, 1408], P('seq', None, 'req'), may hold values from -0.125 to 0.125
- down_weight: bfloat16 [64, 1408, 2048], P('seq', 'req'), may hold values from -0.15625 to 0.15625
- shared_gate: bfloat16 [2048, 2816], P(None, ('req', 'seq')), may hold values from -0.125 to 0.125
- shared_up: bfloat16 [2048, 2816], P(None, ('req', 'seq')), may hold values from -0.125 to 0.125
- shared_down: bfloat16 [2816, 2048], P(('req', 'seq')), may hold values from -0.109375 to 0.109375
- final_gain: float32 [2048], replicated, may hold values from 0.5 to 1.5
- unembed: bfloat16 [102400, 2048], P(('req', 'seq')), may hold values from -0.65115609 to 0.65115609
Outputs:
- layer_out: bfloat16 [64, 2048], P(None, ('req', 'seq'))
- best_logits: float32 [64, 2], replicated
Inputs may be any that keep to these rules, and one draw needn't show every extreme that they name: Request r uses cache positions 0 to lengths[r] - 1, the new token's entry included; in every draw some request's cache is full.
All inputs are finite; a program needn't handle non-finite values.
Results may differ from a plain program's by a relative error of at most 0.0095.
Values may be sent and summed in bfloat16 or wider, within the bound.
A program may use at most 128 MiB of HBM per device.

v0:
```python
import jax
import jax.numpy as jnp
from jax import lax
from jax.sharding import PartitionSpec as P

NEG_FILL = -1e30
NORM_EPS = 1e-06


def combined_all(x, axis, join):
    gathered = jax.tree.map(
        lambda a, kind: lax.all_gather(a.astype(kind), axis),
        x,
        (jnp.bfloat16, jnp.bfloat16, jnp.bfloat16),
    )

    def take(source):
        return jax.tree.map(
            lambda a, own: lax.dynamic_index_in_dim(a, source, 0, False).astype(own.dtype),
            gathered,
            x,
        )

    return lax.fori_loop(
        1, lax.axis_size(axis), lambda source, state: join(state, take(source)), take(0)
    )


def merged_2(x, axis, combine):
    everything = lax.all_gather(x, axis)
    first = everything[0]

    def hop(k, so_far):
        return combine(so_far, everything[k])

    return lax.fori_loop(1, lax.axis_size(axis), hop, first)


def normed(hidden, gain):
    widened = hidden.astype(jnp.float32)
    meansq = jnp.mean(widened * widened, axis=-1, keepdims=True)
    return (widened * lax.rsqrt(meansq + NORM_EPS) * gain).astype(jnp.bfloat16)


def blend(former, latter):
    largest = jnp.maximum(former[0], latter[0])
    former_rescale = jnp.exp(former[0] - largest)
    latter_rescale = jnp.exp(latter[0] - largest)
    totals = former_rescale * former[1] + latter_rescale * latter[1]
    mixes = former_rescale[..., None] * former[2] + latter_rescale[..., None] * latter[2]
    return (largest, totals, mixes)


def best_two(former, latter):
    higher = jnp.maximum(former[:, 0], latter[:, 0])
    lower = jnp.maximum(
        jnp.minimum(former[:, 0], latter[:, 0]), jnp.maximum(former[:, 1], latter[:, 1])
    )
    return jnp.stack([higher, lower], axis=1)


def local(
    residual,
    query_plain,
    query_rotary,
    latent_cache,
    rotary_cache,
    lengths,
    absorb_key,
    absorb_value,
    output_weight,
    middle_gain,
    routes,
    route_weights,
    gate_weight,
    up_weight,
    down_weight,
    shared_gate,
    shared_up,
    shared_down,
    final_gain,
    unembed,
):
    group_rows, head_count, plain_size = query_plain.shape
    block_len = latent_cache.shape[1]
    value_size = absorb_value.shape[2]
    score_scale = (plain_size + query_rotary.shape[2]) ** (-0.5)
    value_wide = absorb_value.astype(jnp.float32)
    query_latent = jnp.einsum(
        "rhn,hnc->rhc", query_plain, absorb_key, preferred_element_type=jnp.float32
    ).astype(jnp.bfloat16)
    scores = jnp.einsum(
        "rhc,rtc->rht", query_latent, latent_cache, preferred_element_type=jnp.float32
    )
    scores = (
        scores
        + jnp.einsum("rhj,rjt->rht", query_rotary, rotary_cache, preferred_element_type=jnp.float32)
    ) * score_scale
    position = lax.axis_index("seq") * block_len + lax.broadcasted_iota(
        jnp.int32, (1, 1, block_len), 2
    )
    usable = position < lengths[:, None, None]
    block_peak = jnp.max(jnp.where(usable, scores, NEG_FILL), axis=2)
    weights = jnp.where(usable, jnp.exp(scores - block_peak[:, :, None]), 0.0).astype(jnp.bfloat16)
    block_total = jnp.sum(weights.astype(jnp.float32), axis=2)
    block_mix = jnp.einsum(
        "rht,rtc->rhc", weights, latent_cache, preferred_element_type=jnp.float32
    )
    merged_peak, merged_total, merged_mix = combined_all(
        (block_peak, block_total, block_mix), "seq", blend
    )
    merged = merged_mix / merged_total[:, :, None]
    merged = jnp.einsum("rhc,hcv->rhv", merged, value_wide, precision=lax.Precision.HIGHEST)
    group_output = merged.astype(jnp.bfloat16).reshape(group_rows, head_count * value_size)
    attn_out = jnp.dot(
        lax.all_gather(group_output, "req", axis=0, tiled=True),
        output_weight,
        preferred_element_type=jnp.float32,
    )
    column_count = residual.shape[1]
    stream_cols = (residual.astype(jnp.float32) + attn_out).astype(jnp.bfloat16)
    stream = lax.all_gather(stream_cols, ("req", "seq"), axis=1, tiled=True)
    expert_in = normed(stream, middle_gain)
    local_count = gate_weight.shape[0]
    expert_index = lax.axis_index("seq") * local_count + lax.broadcasted_iota(
        jnp.int32, (local_count, 1, 1), 0
    )
    route_share = jnp.sum(
        jnp.where(routes[None, :, :] == expert_index, route_weights[None, :, :], 0.0), axis=2
    )
    gate = jnp.einsum("td,edf->etf", expert_in, gate_weight, preferred_element_type=jnp.float32)
    upper = jnp.einsum("td,edf->etf", expert_in, up_weight, preferred_element_type=jnp.float32)
    expert_act = (jax.nn.silu(gate) * upper).astype(jnp.bfloat16)
    expert_back = jnp.einsum(
        "etf,efd->etd", expert_act, down_weight, preferred_element_type=jnp.float32
    )
    shared_gated = jnp.dot(expert_in, shared_gate, preferred_element_type=jnp.float32)
    shared_upper = jnp.dot(expert_in, shared_up, preferred_element_type=jnp.float32)
    shared_act = (jax.nn.silu(shared_gated) * shared_upper).astype(jnp.bfloat16)
    shared_back = jnp.dot(shared_act, shared_down, preferred_element_type=jnp.float32)
    expert_term = jnp.sum(route_share[:, :, None] * expert_back, axis=0) + shared_back
    column_start = lax.axis_index(("req", "seq")) * column_count
    moe = lax.psum(expert_term, ("req", "seq"))
    layer_full = (stream.astype(jnp.float32) + moe).astype(jnp.bfloat16)
    layer_out = lax.dynamic_slice_in_dim(layer_full, column_start, column_count, 1)
    final_in = normed(layer_full, final_gain)
    logits = lax.dot_general(
        final_in, unembed, (((1,), (1,)), ((), ())), preferred_element_type=jnp.float32
    )
    local_best = lax.top_k(logits, 2)[0]
    best_logits = merged_2(local_best, ("req", "seq"), best_two)
    return (layer_out, best_logits)


def solution(mesh):
    in_specs = (
        P(None, ("req", "seq")),
        P("req", None, None),
        P("req", None, None),
        P("req", "seq", None),
        P("req", None, "seq"),
        P("req"),
        P(),
        P(),
        P(None, ("req", "seq")),
        P(),
        P(),
        P(),
        P("seq", None, "req"),
        P("seq", None, "req"),
        P("seq", "req", None),
        P(None, ("req", "seq")),
        P(None, ("req", "seq")),
        P(("req", "seq"), None),
        P(),
        P(("req", "seq"), None),
    )
    out_specs = (P(None, ("req", "seq")), P())
    return jax.shard_map(local, mesh=mesh, in_specs=in_specs, out_specs=out_specs, check_vma=False)
```

profile of v0, /device:TPU:0, one launch (start us, length us, event | category | flops | bytes accessed | tf_op | source)
XLA Modules:
  0.0 327.6 jit_solution(13177338711063554684)
XLA Ops:
  7.2 0.0 copy-start
  7.2 0.0 all-gather.7.cloned.1.call-start
  7.3 0.9 broadcast_compare_fusion
  8.2 0.6 copy-done
  8.8 1.9 fusion.6
  10.7 4.5 %fusion.24 = f32[16,16,384]{2,1,0:T(8,128)S(1)} fusion(bf16[16,384,512]{2,1,0:T(8,128)(2,1)} %param.27, bf16[16,16,512]{2,0,1:T(8,128)(2,1)S(1)} %fusion.6), kind=kOutput, calls=%fused_computation.49 | convolution fusion | flops 100663296 | bytes 6946816 | tf_op jit(solution)/shard_map/rhc,rtc->rht/dot_general | solution.py:92
  15.3 0.0 copy-start.12
  15.3 0.3 select_reduce_fusion
  15.6 1.7 convolution_convert_fusion.1
  17.3 0.0 all-gather.7.cloned.1.call-update
  17.4 0.0 all-reduce.2.cloned.1.call-start
  17.4 0.0 copy-start.6
  17.5 0.2 fusion.34
  17.7 15.8 %all-gather.1 = bf16[128,16]{1,0:T(8,128)(2,1)S(1)} all-gather(bf16[16,16]{1,0:T(8,128)(2,1)S(1)} %fusion.34), channel_id=3, replica_groups=mesh['req'=4,'seq'=8] {'seq'}, dimensions={0}, use_global_device_ids=true | all-gather | bytes 4608 | tf_op jit(solution)/shard_map/all_gather | solution.py:12
  33.5 14.1 %all-gather = bf16[128,16]{1,0:T(8,128)(2,1)S(1)} all-gather(bf16[16,16]{1,0:T(8,128)(2,1)S(1)} %convert_element_type.122), channel_id=2, replica_groups=mesh['req'=4,'seq'=8] {'seq'}, dimensions={0}, use_global_device_ids=true | all-gather | bytes 4608 | tf_op jit(solution)/shard_map/all_gather | solution.py:12
  47.6 0.1 select_reduce_fusion.1
  47.7 2.0 all-gather.7.cloned.1.call-done
  49.6 1.0 slice_convert_fusion
  50.6 8.3 %while.34 = (s32[]{:T(128)}, f32[16,16]{1,0:T(8,128)S(1)}, f32[16,16]{1,0:T(8,128)S(1)}, f32[16,16,512]{2,1,0:T(8,128)S(1)}, bf16[8,16,16]{2,1,0:T(8,128)(2,1)S(...) while((s32[]{:T(128)}, f32[16,16]{1,0:T(8,128)S(1)}, ...), condition=%wide.region_3.4_spmd, body=%wide.region_2.3_spmd.sunk | while | flops 526341 | bytes 1320087 | solution.py:24
  50.7 1.2 fusion.66
  51.9 1.1 fusion.66
  53.1 1.1 fusion.66
  54.3 1.1 fusion.66
  55.4 1.1 fusion.66
  56.6 1.1 fusion.66
  57.8 1.1 fusion.66
  58.9 0.1 broadcast_divide_fusion
  59.0 2.8 fusion.7
  61.8 8.9 %all_gather.33 = bf16[64,2048]{1,0:T(8,128)(2,1)S(1)} all-gather(bf16[16,2048]{1,0:T(8,128)(2,1)S(1)} %bitcast.66), channel_id=1, replica_groups=mesh['req'=4,'seq'=8] {'req'}, dimensions={0}, use_global_device_ids=true | all-gather | bytes 327680 | tf_op jit(solution)/shard_map/all_gather | solution.py:116
  70.8 0.2 fusion.9
  71.0 0.1 copy.44
  71.1 41.6 %all_gather.34 = bf16[64,2048]{0,1:T(8,128)(2,1)S(1)} all-gather(bf16[64,64]{0,1:T(8,128)(2,1)S(1)} %copy.44), channel_id=1, replica_groups=mesh['req'=4,'seq'=8] {'req','seq'}, dimensions={1}, use_global_device_ids=true | all-gather | bytes 270336 | tf_op jit(solution)/shard_map/all_gather | solution.py:122
  112.7 0.2 copy.45
  112.9 0.2 fusion.13
  113.1 0.3 fusion.41
  113.4 7.9 %convolution_bitcast_fusion.1 = f32[8,64,352]{2,1,0:T(8,128)S(1)} fusion(bf16[8,2048,352]{1,2,0:T(8,128)(2,1)} %param.36, bf16[64,2048]{1,0:T(8,128)(2,1)S(1)} %copy.45, f32[2048]{0:T(1024)S(1)} %copy-done.7, f32[64]{0:T(128)S(1)} %add_rsqrt_fusion.1), kind=kOutput, calls=%fused_computation.15 | convolution fusion | flops 738721792 | bytes 12525824 | tf_op jit(solution)/shard_map/td,edf->etf/dot_general | solution.py:131
  121.4 13.4 %multiply_reduce_fusion = f32[64,2048]{1,0:T(8,128)S(1)} fusion(bf16[8,352,2048]{2,1,0:T(8,128)(2,1)} %param.38, f32[8,64]{1,0:T(8,128)S(1)} %select_reduce_fusion.1, bf16[8,2048,352]{1,2,0:T(8,128)(2,1)} %param.37, f32[8,64,352]{2,1,0:T(8,128)S(1)} %convolution_bitcast_fusion.1, bf16[64,2048]{1,0:T(8,128)(2,1)S(1)} %copy.45, f32[2048]{0:T(1024)S(1)} %copy-done.7, ...), kind=kOutput, calls=%fused_computation.12 | convolution fusion | flops 1479966720 | bytes 24586496 | tf_op jit(solution)/shard_map/etf,efd->etd/dot_general | solution.py:134
  134.8 1.4 convolution_add_fusion
  136.2 0.0 all-reduce.2.cloned.1.call-update
  136.3 125.3 %all-reduce.2.cloned.1.call-done = f32[64,2048]{1,0:T(8,128)} async-done(((f32[64,2048]{1,0:T(8,128)}), f32[64,2048]{1,0:T(8,128)}) %all-reduce.2.cloned.1.call-update) | async-done | bytes 524304 | tf_op jit(solution)/shard_map/psum | solution.py:143
  261.6 1.2 fusion.10
  262.8 9.0 %fusion.19 = f32[64,3200]{1,0:T(8,128)S(1)} fusion(bf16[3200,2048]{1,0:T(8,128)(2,1)} %param.43, bf16[64,2048]{1,0:T(8,128)(2,1)S(1)} %get-tuple-element.299, f32[2048]{0:T(1024)S(1)} %copy-done.11, f32[64]{0:T(128)S(1)} %add_rsqrt_fusion), kind=kOutput, calls=%fused_computation.45 | convolution fusion | flops 839385088 | bytes 14196992 | tf_op jit(solution)/shard_map/dot_general | solution.py:147
  271.8 6.6 %top_k.7 = (f32[64,2]{1,0:T(8,128)S(1)}, s32[64,2]{1,0:T(8,128)}) custom-call(f32[64,3200]{1,0:T(8,128)S(1)} %fusion.19), custom_call_target="TopK", called_computations={%compare_greater_than.1.10.clone.clone} | custom-call | tf_op jit(solution)/shard_map/top_k | solution.py:150
  278.4 0.1 copy.46
  278.4 39.6 %all-gather.4 = f32[32,64,2]{1,2,0:T(2,128)S(1)} all-gather(f32[1,64,2]{1,2,0:T(2,128)S(1)} %bitcast.69), channel_id=5, replica_groups=mesh['req'=4,'seq'=8] {'req','seq'}, dimensions={0}, use_global_device_ids=true | all-gather | bytes 16896 | tf_op jit(solution)/shard_map/all_gather | solution.py:30
  318.0 2.0 while.35
  320.0 0.0 copy-start.9
  320.1 0.7 constant_dynamic-slice_fusion
  (134 shorter events, 1.0 us)
Async XLA Ops:
  7.2 1.6 copy-start
  7.2 8.1 %copy-start.8 = (bf16[16,16,64]{2,1,0:T(8,128)(2,1)S(1)}, bf16[16,16,64]{2,1,0:T(8,128)(2,1)}, u32[]{:S(2)}) copy-start(bf16[16,16,64]{2,1,0:T(8,128)(2,1)} %param.26) | copy-start | bytes 98308
  7.2 8.1 %copy-start.3 = (bf16[16,64,384]{2,1,0:T(8,128)(2,1)S(1)}, bf16[16,64,384]{2,1,0:T(8,128)(2,1)}, u32[]{:S(2)}) copy-start(bf16[16,64,384]{2,1,0:T(8,128)(2,1)} %param.28) | copy-start | bytes 2359300
  7.2 42.4 %all-gather.7.cloned.1.call-start = ((), (), s32[]{:S(2)}) async-start(), calls=%async_computation.1 | async-start | bytes 2359296 | tf_op jit(solution)/shard_map/all_gather | solution.py:12
  7.3 8.4 %copy-start.2 = (bf16[16,384,512]{2,1,0:T(8,128)(2,1)S(1)}, bf16[16,384,512]{2,1,0:T(8,128)(2,1)}, u32[]{:S(2)}) copy-start(bf16[16,384,512]{2,1,0:T(8,128)(2,1)} %param.27) | copy-start | bytes 18874372
  15.3 32.3 %copy-start.12 = (f32[64,6]{0,1:T(8,128)S(1)}, f32[64,6]{0,1:T(8,128)}, u32[]{:S(2)}) copy-start(f32[64,6]{0,1:T(8,128)} %param.35) | copy-start | bytes 4612
  15.3 32.3 %copy-start.13 = (s32[64,6]{0,1:T(8,128)S(1)}, s32[64,6]{0,1:T(8,128)}, u32[]{:S(2)}) copy-start(s32[64,6]{0,1:T(8,128)} %param.34) | copy-start | bytes 4612
  17.4 244.2 %all-reduce.2.cloned.1.call-start = ((), (), s32[]{:S(2)}) async-start(), calls=%async_computation | async-start | bytes 1048576 | tf_op jit(solution)/shard_map/psum | solution.py:143
  17.4 53.4 %copy-start.6 = (bf16[2048,64]{0,1:T(8,128)(2,1)S(1)}, bf16[2048,64]{0,1:T(8,128)(2,1)}, u32[]{:S(2)}) copy-start(bf16[2048,64]{0,1:T(8,128)(2,1)} %param.32) | copy-start | bytes 786436
  17.4 53.3 %copy-start.10 = (bf16[64,64]{1,0:T(8,128)(2,1)S(1)}, bf16[64,64]{1,0:T(8,128)(2,1)}, u32[]{:S(2)}) copy-start(bf16[64,64]{1,0:T(8,128)(2,1)} %param.24) | copy-start | bytes 24580
  50.6 62.5 %copy-start.7 = (f32[2048]{0:T(1024)S(1)}, f32[2048]{0:T(1024)}, u32[]{:S(2)}) copy-start(f32[2048]{0:T(1024)} %param.33) | copy-start | bytes 24580
  50.6 62.5 %copy-start.14 = (bf16[2048,88]{0,1:T(8,128)(2,1)S(1)}, bf16[2048,88]{0,1:T(8,128)(2,1)}, u32[]{:S(2)}) copy-start(bf16[2048,88]{0,1:T(8,128)(2,1)} %param.39) | copy-start | bytes 1081348
  121.4 13.4 %copy-start.4 = (bf16[88,2048]{1,0:T(8,128)(2,1)S(1)}, bf16[88,2048]{1,0:T(8,128)(2,1)}, u32[]{:S(2)}) copy-start(bf16[88,2048]{1,0:T(8,128)(2,1)} %param.41) | copy-start | bytes 1081348
  121.4 13.4 %copy-start.5 = (bf16[2048,88]{0,1:T(8,128)(2,1)S(1)}, bf16[2048,88]{0,1:T(8,128)(2,1)}, u32[]{:S(2)}) copy-start(bf16[2048,88]{0,1:T(8,128)(2,1)} %param.40) | copy-start | bytes 1081348
  121.4 141.4 %copy-start.11 = (f32[2048]{0:T(1024)S(1)}, f32[2048]{0:T(1024)}, u32[]{:S(2)}) copy-start(f32[2048]{0:T(1024)} %param.42) | copy-start | bytes 24580
  262.8 58.0 %copy-start.1 = (bf16[16,128,512]{2,1,0:T(8,128)(2,1)S(1)}, bf16[16,128,512]{2,1,0:T(8,128)(2,1)}, u32[]{:S(2)}) copy-start(bf16[16,128,512]{2,1,0:T(8,128)(2,1)} %param.30) | copy-start | bytes 6291460
  320.0 0.7 copy-start.9
Sparse Core Ops, SparseCore 0:
  17.5 32.0 all-gather.6
  136.4 125.1 all-reduce.1
where the time goes:
time: 328 us
  waiting for transfers between devices  127 us (39%)
  blocking collectives  120 us (37%)
  matrix products  43.5 us (13%)
  other arithmetic  18.8 us (6%)
  between operations  14.4 us (4%)
    psum x1, waiting for transfers between devices, local(): moe = lax.psum(expert_term, ('req', 'seq'))  125 us
    all_gather x1, blocking collectives, local(): stream = lax.all_gather(stream_cols, ('req', 'seq'), axis=1, tiled=True)  41.6 us
    all_gather x1, blocking collectives, merged_2(): everything = lax.all_gather(x, axis)  39.6 us
    all_gather x2, blocking collectives, combined_all(): lax.all_gather(a.astype(kind), axis)  29.9 us
    dot_general x1, matrix products, local(): jnp.einsum('etf,efd->etd', expert_act, down_weight, preferred_element_typ...  13.4 us
    dot_general x1, matrix products, local(): lax.dot_general(final_in, unembed, (((1,), (1,)), ((), ())), preferred_el...  8.97 us
    all_gather x1, blocking collectives, local(): lax.all_gather(group_output, 'req', axis=0, tiled=True)  8.95 us
    dot_general x1, matrix products, local(): jnp.einsum('td,edf->etf', expert_in, gate_weight, preferred_element_type=...  7.94 us
  transfers between devices with their start and end apart: 2, of which 2 were waited for; matrix products, arithmetic and copies ran while one was open for 0% of the time, Pallas kernels for 0%

commit v1 on v0

--- a/solution.py
+++ b/solution.py
@@ -140,7 +140,7 @@
     shared_back = jnp.dot(shared_act, shared_down, preferred_element_type=jnp.float32)
     expert_term = jnp.sum(route_share[:, :, None] * expert_back, axis=0) + shared_back
     column_start = lax.axis_index(("req", "seq")) * column_count
-    moe = lax.psum(expert_term, ("req", "seq"))
+    moe = lax.psum(lax.psum(expert_term, "seq"), "req")
     layer_full = (stream.astype(jnp.float32) + moe).astype(jnp.bfloat16)
     layer_out = lax.dynamic_slice_in_dim(layer_full, column_start, column_count, 1)
     final_in = normed(layer_full, final_gain)

time: 328 us -> 305 us (0.930)
  waiting for transfers between devices: 127 us -> 103 us
    psum x1 -> x2, waiting for transfers between devices: 125 us -> 101 us  [local(): moe = lax.psum(lax.psum(expert_term, 'seq'), 'req')]
  transfers between devices with their start and end apart: 2 -> 3, of which waited for: 2 -> 3; matrix products, arithmetic and copies ran while one was open for 0% -> 0% of each run, Pallas kernels for 0% -> 0%
where the time goes in v1:
time: 305 us; the launch traced here: 304 us
  blocking collectives  121 us (40%)
  waiting for transfers between devices  103 us (34%)
  matrix products  43.5 us (14%)
  other arithmetic  18.8 us (6%)
  between operations  14.1 us (5%)
    psum x2, waiting for transfers between devices, local(): moe = lax.psum(lax.psum(expert_term, 'seq'), 'req')  101 us
    all_gather x1, blocking collectives, local(): stream = lax.all_gather(stream_cols, ('req', 'seq'), axis=1, tiled=True)  41.6 us
    all_gather x1, blocking collectives, merged_2(): everything = lax.all_gather(x, axis)  40.6 us
    all_gather x2, blocking collectives, combined_all(): lax.all_gather(a.astype(kind), axis)  29.9 us
    dot_general x1, matrix products, local(): jnp.einsum('etf,efd->etd', expert_act, down_weight, preferred_element_typ...  13.4 us
    dot_general x1, matrix products, local(): lax.dot_general(final_in, unembed, (((1,), (1,)), ((), ())), preferred_el...  8.97 us
    all_gather x1, blocking collectives, local(): lax.all_gather(group_output, 'req', axis=0, tiled=True)  8.95 us
    dot_general x1, matrix products, local(): jnp.einsum('td,edf->etf', expert_in, gate_weight, preferred_element_type=...  7.94 us
  transfers between devices with their start and end apart: 3, of which 3 were waited for; matrix products, arithmetic and copies ran while one was open for 0% of the time, Pallas kernels for 0%

profile of v1, /device:TPU:0, one launch (start us, length us, event | category | flops | bytes accessed | tf_op | source)
XLA Modules:
  0.0 304.1 jit_solution(14796027594427956927)
XLA Ops:
  7.2 0.0 all-gather.7.cloned.1.call-start
  7.3 0.9 broadcast_compare_fusion
  8.2 0.6 copy-done
  8.8 1.9 fusion.6
  10.7 4.5 %fusion.24 = f32[16,16,384]{2,1,0:T(8,128)S(1)} fusion(bf16[16,384,512]{2,1,0:T(8,128)(2,1)} %param.27, bf16[16,16,512]{2,0,1:T(8,128)(2,1)S(1)} %fusion.6), kind=kOutput, calls=%fused_computation.49 | convolution fusion | flops 100663296 | bytes 6946816 | tf_op jit(solution)/shard_map/rhc,rtc->rht/dot_general | solution.py:92
  15.3 0.0 copy-start.12
  15.3 0.3 select_reduce_fusion
  15.6 1.7 convolution_convert_fusion.1
  17.3 0.0 all-gather.7.cloned.1.call-update
  17.4 0.0 all-reduce.3.cloned.1.call-start
  17.5 0.2 fusion.34
  17.7 15.8 %all-gather.1 = bf16[128,16]{1,0:T(8,128)(2,1)S(1)} all-gather(bf16[16,16]{1,0:T(8,128)(2,1)S(1)} %fusion.34), channel_id=3, replica_groups=mesh['req'=4,'seq'=8] {'seq'}, dimensions={0}, use_global_device_ids=true | all-gather | bytes 4608 | tf_op jit(solution)/shard_map/all_gather | solution.py:12
  33.5 14.1 %all-gather = bf16[128,16]{1,0:T(8,128)(2,1)S(1)} all-gather(bf16[16,16]{1,0:T(8,128)(2,1)S(1)} %convert_element_type.122), channel_id=2, replica_groups=mesh['req'=4,'seq'=8] {'seq'}, dimensions={0}, use_global_device_ids=true | all-gather | bytes 4608 | tf_op jit(solution)/shard_map/all_gather | solution.py:12
  47.6 0.1 select_reduce_fusion.1
  47.7 2.0 all-gather.7.cloned.1.call-done
  49.6 1.0 slice_convert_fusion
  50.6 8.3 %while.34 = (s32[]{:T(128)}, f32[16,16]{1,0:T(8,128)S(1)}, f32[16,16]{1,0:T(8,128)S(1)}, f32[16,16,512]{2,1,0:T(8,128)S(1)}, bf16[8,16,16]{2,1,0:T(8,128)(2,1)S(...) while((s32[]{:T(128)}, f32[16,16]{1,0:T(8,128)S(1)}, ...), condition=%wide.region_3.4_spmd, body=%wide.region_2.3_spmd.sunk | while | flops 526341 | bytes 1320087 | solution.py:24
  50.7 1.2 fusion.66
  51.9 1.1 fusion.66
  53.1 1.1 fusion.66
  54.3 1.1 fusion.66
  55.4 1.1 fusion.66
  56.6 1.1 fusion.66
  57.8 1.1 fusion.66
  58.9 0.1 broadcast_divide_fusion
  59.0 2.8 fusion.7
  61.8 8.9 %all_gather.33 = bf16[64,2048]{1,0:T(8,128)(2,1)S(1)} all-gather(bf16[16,2048]{1,0:T(8,128)(2,1)S(1)} %bitcast.66), channel_id=1, replica_groups=mesh['req'=4,'seq'=8] {'req'}, dimensions={0}, use_global_device_ids=true | all-gather | bytes 327680 | tf_op jit(solution)/shard_map/all_gather | solution.py:116
  70.8 0.2 fusion.9
  71.0 0.1 copy.44
  71.1 41.6 %all_gather.34 = bf16[64,2048]{0,1:T(8,128)(2,1)S(1)} all-gather(bf16[64,64]{0,1:T(8,128)(2,1)S(1)} %copy.44), channel_id=1, replica_groups=mesh['req'=4,'seq'=8] {'req','seq'}, dimensions={1}, use_global_device_ids=true | all-gather | bytes 270336 | tf_op jit(solution)/shard_map/all_gather | solution.py:122
  112.7 0.2 copy.45
  112.9 0.2 fusion.13
  113.1 0.3 fusion.41
  113.4 7.9 %convolution_bitcast_fusion.1 = f32[8,64,352]{2,1,0:T(8,128)S(1)} fusion(bf16[8,2048,352]{1,2,0:T(8,128)(2,1)} %param.36, bf16[64,2048]{1,0:T(8,128)(2,1)S(1)} %copy.45, f32[2048]{0:T(1024)S(1)} %copy-done.7, f32[64]{0:T(128)S(1)} %add_rsqrt_fusion.1), kind=kOutput, calls=%fused_computation.15 | convolution fusion | flops 738721792 | bytes 12525824 | tf_op jit(solution)/shard_map/td,edf->etf/dot_general | solution.py:131
  121.4 13.4 %multiply_reduce_fusion = f32[64,2048]{1,0:T(8,128)S(1)} fusion(bf16[8,352,2048]{2,1,0:T(8,128)(2,1)} %param.38, f32[8,64]{1,0:T(8,128)S(1)} %select_reduce_fusion.1, bf16[8,2048,352]{1,2,0:T(8,128)(2,1)} %param.37, f32[8,64,352]{2,1,0:T(8,128)S(1)} %convolution_bitcast_fusion.1, bf16[64,2048]{1,0:T(8,128)(2,1)S(1)} %copy.45, f32[2048]{0:T(1024)S(1)} %copy-done.7, ...), kind=kOutput, calls=%fused_computation.12 | convolution fusion | flops 1479966720 | bytes 24586496 | tf_op jit(solution)/shard_map/etf,efd->etd/dot_general | solution.py:134
  134.8 1.4 convolution_add_fusion
  136.2 0.0 all-reduce.3.cloned.1.call-update
  136.3 0.0 all-reduce.5.cloned.1.call-start
  136.3 53.5 %all-reduce.3.cloned.1.call-done = f32[64,2048]{1,0:T(8,128)} async-done(((f32[64,2048]{1,0:T(8,128)}), f32[64,2048]{1,0:T(8,128)}) %all-reduce.3.cloned.1.call-update) | async-done | bytes 524304 | tf_op jit(solution)/shard_map/psum | solution.py:143
  189.8 0.0 all-reduce.5.cloned.1.call-update
  189.8 47.6 %all-reduce.5.cloned.1.call-done = f32[64,2048]{1,0:T(8,128)} async-done(((f32[64,2048]{1,0:T(8,128)}), f32[64,2048]{1,0:T(8,128)}) %all-reduce.5.cloned.1.call-update) | async-done | bytes 524304 | tf_op jit(solution)/shard_map/psum | solution.py:143
  237.4 1.2 fusion.10
  238.7 9.0 %fusion.19 = f32[64,3200]{1,0:T(8,128)S(1)} fusion(bf16[3200,2048]{1,0:T(8,128)(2,1)} %param.43, bf16[64,2048]{1,0:T(8,128)(2,1)S(1)} %get-tuple-element.299, f32[2048]{0:T(1024)S(1)} %copy-done.11, f32[64]{0:T(128)S(1)} %add_rsqrt_fusion), kind=kOutput, calls=%fused_computation.45 | convolution fusion | flops 839385088 | bytes 14196992 | tf_op jit(solution)/shard_map/dot_general | solution.py:147
  247.6 6.6 %top_k.7 = (f32[64,2]{1,0:T(8,128)S(1)}, s32[64,2]{1,0:T(8,128)}) custom-call(f32[64,3200]{1,0:T(8,128)S(1)} %fusion.19), custom_call_target="TopK", called_computations={%compare_greater_than.1.11.clone.clone} | custom-call | tf_op jit(solution)/shard_map/top_k | solution.py:150
  254.2 0.1 copy.46
  254.3 40.6 %all-gather.4 = f32[32,64,2]{1,2,0:T(2,128)S(1)} all-gather(f32[1,64,2]{1,2,0:T(2,128)S(1)} %bitcast.69), channel_id=5, replica_groups=mesh['req'=4,'seq'=8] {'req','seq'}, dimensions={0}, use_global_device_ids=true | all-gather | bytes 16896 | tf_op jit(solution)/shard_map/all_gather | solution.py:30
  294.9 2.0 while.35
  296.9 0.7 constant_dynamic-slice_fusion
  (137 shorter events, 1.0 us)
Async XLA Ops:
  7.2 1.6 copy-start
  7.2 8.1 %copy-start.8 = (bf16[16,16,64]{2,1,0:T(8,128)(2,1)S(1)}, bf16[16,16,64]{2,1,0:T(8,128)(2,1)}, u32[]{:S(2)}) copy-start(bf16[16,16,64]{2,1,0:T(8,128)(2,1)} %param.26) | copy-start | bytes 98308
  7.2 8.1 %copy-start.3 = (bf16[16,64,384]{2,1,0:T(8,128)(2,1)S(1)}, bf16[16,64,384]{2,1,0:T(8,128)(2,1)}, u32[]{:S(2)}) copy-start(bf16[16,64,384]{2,1,0:T(8,128)(2,1)} %param.28) | copy-start | bytes 2359300
  7.2 42.4 %all-gather.7.cloned.1.call-start = ((), (), s32[]{:S(2)}) async-start(), calls=%async_computation.2 | async-start | bytes 2359296 | tf_op jit(solution)/shard_map/all_gather | solution.py:12
  7.3 8.4 %copy-start.2 = (bf16[16,384,512]{2,1,0:T(8,128)(2,1)S(1)}, bf16[16,384,512]{2,1,0:T(8,128)(2,1)}, u32[]{:S(2)}) copy-start(bf16[16,384,512]{2,1,0:T(8,128)(2,1)} %param.27) | copy-start | bytes 18874372
  15.3 32.3 %copy-start.12 = (f32[64,6]{0,1:T(8,128)S(1)}, f32[64,6]{0,1:T(8,128)}, u32[]{:S(2)}) copy-start(f32[64,6]{0,1:T(8,128)} %param.35) | copy-start | bytes 4612
  15.3 32.3 %copy-start.13 = (s32[64,6]{0,1:T(8,128)S(1)}, s32[64,6]{0,1:T(8,128)}, u32[]{:S(2)}) copy-start(s32[64,6]{0,1:T(8,128)} %param.34) | copy-start | bytes 4612
  17.4 172.4 %all-reduce.3.cloned.1.call-start = ((), (), s32[]{:S(2)}) async-start(), calls=%async_computation | async-start | bytes 1048576 | tf_op jit(solution)/shard_map/psum | solution.py:143
  17.4 53.4 %copy-start.6 = (bf16[2048,64]{0,1:T(8,128)(2,1)S(1)}, bf16[2048,64]{0,1:T(8,128)(2,1)}, u32[]{:S(2)}) copy-start(bf16[2048,64]{0,1:T(8,128)(2,1)} %param.32) | copy-start | bytes 786436
  17.4 53.3 %copy-start.10 = (bf16[64,64]{1,0:T(8,128)(2,1)S(1)}, bf16[64,64]{1,0:T(8,128)(2,1)}, u32[]{:S(2)}) copy-start(bf16[64,64]{1,0:T(8,128)(2,1)} %param.24) | copy-start | bytes 24580
  50.6 62.5 %copy-start.7 = (f32[2048]{0:T(1024)S(1)}, f32[2048]{0:T(1024)}, u32[]{:S(2)}) copy-start(f32[2048]{0:T(1024)} %param.33) | copy-start | bytes 24580
  50.6 62.5 %copy-start.14 = (bf16[2048,88]{0,1:T(8,128)(2,1)S(1)}, bf16[2048,88]{0,1:T(8,128)(2,1)}, u32[]{:S(2)}) copy-start(bf16[2048,88]{0,1:T(8,128)(2,1)} %param.39) | copy-start | bytes 1081348
  121.4 13.4 %copy-start.4 = (bf16[88,2048]{1,0:T(8,128)(2,1)S(1)}, bf16[88,2048]{1,0:T(8,128)(2,1)}, u32[]{:S(2)}) copy-start(bf16[88,2048]{1,0:T(8,128)(2,1)} %param.41) | copy-start | bytes 1081348
  121.4 13.4 %copy-start.5 = (bf16[2048,88]{0,1:T(8,128)(2,1)S(1)}, bf16[2048,88]{0,1:T(8,128)(2,1)}, u32[]{:S(2)}) copy-start(bf16[2048,88]{0,1:T(8,128)(2,1)} %param.40) | copy-start | bytes 1081348
  121.4 117.3 %copy-start.11 = (f32[2048]{0:T(1024)S(1)}, f32[2048]{0:T(1024)}, u32[]{:S(2)}) copy-start(f32[2048]{0:T(1024)} %param.42) | copy-start | bytes 24580
  136.3 101.2 %all-reduce.5.cloned.1.call-start = ((), (), s32[]{:S(2)}) async-start(), calls=%async_computation.1 | async-start | bytes 1048576 | tf_op jit(solution)/shard_map/psum | solution.py:143
  238.6 58.9 %copy-start.1 = (bf16[16,128,512]{2,1,0:T(8,128)(2,1)S(1)}, bf16[16,128,512]{2,1,0:T(8,128)(2,1)}, u32[]{:S(2)}) copy-start(bf16[16,128,512]{2,1,0:T(8,128)(2,1)} %param.30) | copy-start | bytes 6291460
  296.9 0.7 copy-start.9
Sparse Core Ops, SparseCore 0:
  17.5 32.0 all-gather.6
  136.4 53.3 all-reduce.2
  193.1 44.3 all-reduce.4
